TPU v7x, 512 devices: a whole 4x4x16 slice. The times are simulated.
512 devices in a mesh: grp: 16 (over y, x), dev: 32 (over z, core).
Axes of the slice: x: 4, y: 4, z: 16, core: 2. Of those that a mesh axis runs over, the one named last changes fastest.
Arguments:
- points: float32 [3, 524288], P(None, ('grp', 'dev')), may hold values from 0 to 2
- charges: float32 [16, 524288], P(None, ('grp', 'dev')), may hold values from -6 to 6
- morton: int32 [524288], P(('grp', 'dev')), may hold values from 0 to 1023, as said below
- neighbours: int32 [2048, 8], P(('grp', 'dev')), may hold values from 0 to 2047, as said below
- counts: int32 [2048], P(('grp', 'dev')), may hold values from 1 to 8
- skel_leaf: float32 [3, 524288], P(None, ('grp', 'dev')), may hold values from 0 to 2
- skel_block: float32 [3, 131072], P(None, ('grp', 'dev')), may hold values from 0 to 2
- skel_group: float32 [3, 4096], replicated, may hold values from 0 to 2
Outputs:
- potential: float32 [16, 524288], P(None, ('grp', 'dev'))
Inputs may be any that keep to these rules, and one draw needn't show every extreme that they name: `morton`: each aligned run of 1024 entries is a permutation of 0 to 1023. `neighbours`: entry [q, k] is a leaf other than q, at most 4 leaves away from q; only slots k < counts[q] are used.
All inputs are finite; a program needn't handle non-finite values.
Results may differ from a plain program's by a relative error of at most 0.0003.
Values sent between devices are 32-bit elements; how exact they have to be, the bound alone decides.
No kernel may reach another device: no remote copies, remote signals or barrier semaphores. Data moves between devices by JAX's collectives and lax.ppermute only.
A program may use at most 64 MiB of HBM per device.

v0:
```python
import math
import jax
import jax.numpy as jnp
from jax import lax
from jax.sharding import PartitionSpec as P

width_sq = 0.1
gain_factor = 5.0


def extended_2(cells, sides, width):
    for axis, dim in sides:
        count = lax.axis_size(axis)
        ends = count - 1
        head = lax.slice_in_dim(cells, 0, width, axis=dim)
        tail = lax.slice_in_dim(cells, cells.shape[dim] - width, cells.shape[dim], axis=dim)
        cells = jnp.concatenate(
            [
                lax.ppermute(tail, axis, [(i, (i + 1) % count) for i in range(ends)]),
                cells,
                lax.ppermute(head, axis, [((i + 1) % count, i) for i in range(ends)]),
            ],
            axis=dim,
        )
    return cells


def kernel_tile(source, target):
    distance = (source[0][:, None] - target[0][None, :]) ** 2
    distance = distance + (source[1][:, None] - target[1][None, :]) ** 2
    distance = distance + (source[2][:, None] - target[2][None, :]) ** 2
    return jnp.exp(-distance / width_sq)


def translate(values, source, target, term_count):
    product = jnp.dot(
        values,
        kernel_tile(source, target),
        precision=lax.Precision.HIGHEST,
        preferred_element_type=jnp.float32,
    )
    return gain_factor / math.sqrt(term_count) * product


def far_sum(running, weights, skeleton, target, own_member, skel_rank, term_count):
    span_cols = weights.shape[1]
    block_cols = min(skel_rank, span_cols)

    def one_block(block_index, partial_value):
        column = block_index * block_cols
        piece_w = lax.dynamic_slice_in_dim(weights, column, block_cols, 1)
        piece_s = lax.dynamic_slice_in_dim(skeleton, column, block_cols, 1)
        member = column // skel_rank
        keep_mask = jnp.where(member == own_member, 0.0, 1.0)
        return partial_value + keep_mask * translate(piece_w, piece_s, target, term_count)

    return lax.fori_loop(0, span_cols // block_cols, one_block, running)


def body(points, charges, morton, neighbours, counts, skel_leaf, skel_block, skel_group):
    n_groups = lax.axis_size("grp")
    n_blocks = lax.axis_size("dev")
    vectors, block_pts = charges.shape
    leaf_count = counts.shape[0]
    leaf_size = block_pts // leaf_count
    skel_rank = skel_block.shape[1]
    slot_total = neighbours.shape[1]
    group_id = lax.axis_index("grp")
    member_id = lax.axis_index("dev")
    block_id = group_id * n_blocks + member_id
    sorted_pts = jnp.take(points, morton, axis=1)
    sorted_chg = jnp.take(charges, morton, axis=1)
    leaf_pts = sorted_pts.reshape(3, leaf_count, leaf_size).transpose(1, 0, 2)
    leaf_chg = sorted_chg.reshape(vectors, leaf_count, leaf_size).transpose(1, 0, 2)
    leaf_skel = skel_leaf.reshape(3, leaf_count, skel_rank).transpose(1, 0, 2)
    leaf_weights = lax.map(
        lambda inputs: translate(inputs[0], inputs[1], inputs[2], leaf_size),
        (leaf_chg, leaf_pts, leaf_skel),
    )
    lifted = lax.map(
        lambda inputs: translate(inputs[0], inputs[1], skel_block, leaf_count * skel_rank),
        (leaf_weights, leaf_skel),
    )
    block_weights = jnp.sum(lifted, axis=0)
    own_group = lax.dynamic_slice_in_dim(skel_group, group_id * skel_rank, skel_rank, 1)
    raised = translate(block_weights, skel_block, own_group, n_blocks * skel_rank)
    empty = jnp.zeros((vectors, skel_rank), jnp.float32)
    group_terms = (n_groups - 1) * skel_rank
    group_weights = lax.psum(raised, "dev")
    group_field = far_sum(
        empty,
        lax.all_gather(group_weights, "grp", axis=1, tiled=True),
        skel_group,
        own_group,
        group_id,
        skel_rank,
        group_terms,
    )
    peer_field = far_sum(
        empty,
        lax.all_gather(block_weights, "dev", axis=1, tiled=True),
        lax.all_gather(skel_block, "dev", axis=1, tiled=True),
        skel_block,
        member_id,
        skel_rank,
        (n_blocks - 1) * skel_rank,
    )
    block_field = peer_field + translate(group_field, own_group, skel_block, skel_rank)
    leaf_field = lax.map(
        lambda target: translate(block_field, skel_block, target, skel_rank), leaf_skel
    )
    stacked = jnp.concatenate([sorted_pts, sorted_chg], axis=0)
    extended = extended_2(stacked, ((("grp", "dev"), 1),), block_pts)
    ext_leaves = extended.reshape(3 + vectors, 3 * leaf_count, leaf_size).transpose(1, 0, 2)
    first_leaf = block_id * leaf_count - leaf_count

    def near_leaf(inputs):
        own_pts, own_chg, own_field, own_skel, row_nbr, row_count = inputs
        direct = translate(own_chg, own_pts, own_pts, leaf_size)
        direct = direct + translate(own_field, own_skel, own_pts, skel_rank)

        def one_slot(slot_index, running):
            source = lax.dynamic_index_in_dim(
                ext_leaves, row_nbr[slot_index] - first_leaf, 0, keepdims=False
            )
            tile_term = translate(source[3:], source[:3], own_pts, leaf_size)
            return running + jnp.where(slot_index < row_count, tile_term, jnp.zeros_like(tile_term))

        return lax.fori_loop(0, slot_total, one_slot, direct)

    potential = lax.map(near_leaf, (leaf_pts, leaf_chg, leaf_field, leaf_skel, neighbours, counts))
    return potential.transpose(1, 0, 2).reshape(vectors, block_pts)


def solution(mesh):
    return jax.shard_map(
        body,
        mesh=mesh,
        in_specs=(
            P(None, ("grp", "dev")),
            P(None, ("grp", "dev")),
            P(("grp", "dev")),
            P(("grp", "dev"), None),
            P(("grp", "dev")),
            P(None, ("grp", "dev")),
            P(None, ("grp", "dev")),
            P(),
        ),
        out_specs=P(None, ("grp", "dev")),
        check_vma=False,
    )
```

profile of v0, /device:TPU:8, one launch (start us, length us, event | category | flops | bytes accessed | tf_op | source)
XLA Modules:
  0.0 328.9 jit_solution(2411669421259678028)
XLA Ops:
  0.8 0.9 copy.25
  1.7 2.8 gather_fusion.1
  5.8 2.8 gather_fusion
  9.0 12.9 %collective-permute-start.1 = (f32[19,1024]{1,0:T(8,128)S(1)}, f32[19,1024]{1,0:T(8,128)S(1)}, u32[]{:S(2)}, u32[]{:S(2)}) collective-permute-start(f32[19,1024]{1,0:T(8,128)S(1)} %pad_maximum_fusion.1), channel_id=1, source_target_pairs={{1,0},{2,1},{3,2},{4,3},{5,4},{6,5},{7,6},{8,7},{9,8},{10,9},{11,1... | collective-permute-start | bytes 233480 | tf_op jit(solution)/shard_map/ppermute | solution.py:21
  21.9 1.9 collective-permute-start
  24.6 27.1 %all_gather.10 = f32[3,8192]{1,0:T(4,128)S(1)} all-gather(f32[3,256]{1,0:T(4,128)S(1)} %copy-done), channel_id=1, replica_groups=mesh['grp'=16,'dev'=32] {'dev'}, dimensions={1}, use_global_device_ids=true | all-gather | bytes 101376 | tf_op jit(solution)/shard_map/all_gather | solution.py:102
  52.8 1.6 while.85
  54.5 1.7 while.86
  56.2 30.2 %all_gather.9 = f32[16,8192]{1,0:T(8,128)S(1)} all-gather(f32[16,256]{1,0:T(8,128)S(1)} %reduce_sum.9), channel_id=1, replica_groups=mesh['grp'=16,'dev'=32] {'dev'}, dimensions={1}, use_global_device_ids=true | all-gather | bytes 540672 | tf_op jit(solution)/shard_map/all_gather | solution.py:101
  88.3 90.3 %psum.7 = f32[16,256]{1,0:T(8,128)S(1)} all-reduce(f32[16,256]{1,0:T(8,128)S(1)} %convolution_multiply_fusion.7), channel_id=1, replica_groups=mesh['grp'=16,'dev'=32] {'dev'}, use_global_device_ids=true, to_apply=%region_7.8 | all-reduce | flops 4096 | bytes 32768 | tf_op jit(solution)/shard_map/psum | solution.py:89
  178.7 24.5 %all_gather.11 = f32[16,4096]{1,0:T(8,128)S(1)} all-gather(f32[16,256]{1,0:T(8,128)S(1)} %psum.7), channel_id=1, replica_groups=mesh['grp'=16,'dev'=32] {'grp'}, dimensions={1}, use_global_device_ids=true | all-gather | bytes 278528 | tf_op jit(solution)/shard_map/all_gather | solution.py:92
  203.1 21.3 %while.91 = (s32[]{:T(128)}, f32[16,256]{1,0:T(8,128)S(1)}, f32[16,4096]{1,0:T(8,128)S(1)}, f32[3,4096]{1,0:T(4,128)}, f32[3,256]{1,0:T(4,128)S(1)}, /*index=5*/...) while((s32[]{:T(128)}, f32[16,256]{1,0:T(8,128)S(1)}, ...), condition=%wide.region_9.10_spmd.clone, body=%wide.region_8.9_spmd.clone.sunk | while | flops 13250586 | bytes 68032 | solution.py:57
  203.1 0.9 constant_dynamic-slice_fusion.38
  204.5 0.9 constant_dynamic-slice_fusion.38
  205.8 0.9 constant_dynamic-slice_fusion.38
  207.1 0.9 constant_dynamic-slice_fusion.38
  208.5 0.9 constant_dynamic-slice_fusion.38
  209.8 0.9 constant_dynamic-slice_fusion.38
  211.1 0.9 constant_dynamic-slice_fusion.38
  212.5 0.9 constant_dynamic-slice_fusion.38
  213.8 0.9 constant_dynamic-slice_fusion.38
  215.1 0.9 constant_dynamic-slice_fusion.38
  216.5 0.9 constant_dynamic-slice_fusion.38
  217.8 0.9 constant_dynamic-slice_fusion.38
  221.8 0.9 constant_dynamic-slice_fusion.38
  224.4 17.1 %while.90 = (s32[]{:T(128)}, f32[16,256]{1,0:T(8,128)S(1)}, f32[16,8192]{1,0:T(8,128)S(1)}, f32[3,8192]{1,0:T(4,128)S(1)}, f32[3,256]{1,0:T(4,128)S(1)}, /*index...) while((s32[]{:T(128)}, f32[16,256]{1,0:T(8,128)S(1)}, ...), condition=%wide.region_6.7_spmd.clone, body=%wide.region_5.6_spmd.clone.sunk | while | flops 13250586 | bytes 68032 | solution.py:57
  241.9 1.8 while.87
  244.7 83.6 %while.89 = (s32[]{:T(128)}, f32[4,16,256]{2,1,0:T(8,128)S(1)}, f32[4,16,256]{2,1,0:T(8,128)S(1)}, f32[4,3,256]{2,1,0:T(4,128)S(1)}, f32[4,16,256]{2,1,0:T(8,128...) while((s32[]{:T(128)}, f32[4,16,256]{2,1,0:T(8,128)S(1)}, ...), condition=%wide.region_15.16_spmd, body=%wide.region_12.15_spmd.sunk | while | flops 39735312 | bytes 213682 | solution.py:131
  246.8 18.8 %while.92 = (s32[]{:T(128)}, f32[16,256]{1,0:T(8,128)S(1)}, s32[]{:T(128)}, s32[8]{0:T(128)S(1)}, s32[]{:T(128)}, /*index=5*/f32[12,19,256]{2,1,0:T(8,128)S(1)},...) while((s32[]{:T(128)}, f32[16,256]{1,0:T(8,128)S(1)}, ...), condition=%wide.region_14.14_spmd, body=%wide.region_13.13_spmd.sunk | while | flops 13250570 | bytes 67841 | solution.py:129
  267.6 18.8 %while.92 = (s32[]{:T(128)}, f32[16,256]{1,0:T(8,128)S(1)}, s32[]{:T(128)}, s32[8]{0:T(128)S(1)}, s32[]{:T(128)}, /*index=5*/f32[12,19,256]{2,1,0:T(8,128)S(1)},...) while((s32[]{:T(128)}, f32[16,256]{1,0:T(8,128)S(1)}, ...), condition=%wide.region_14.14_spmd, body=%wide.region_13.13_spmd.sunk | while | flops 13250570 | bytes 67841 | solution.py:129
  288.5 18.8 %while.92 = (s32[]{:T(128)}, f32[16,256]{1,0:T(8,128)S(1)}, s32[]{:T(128)}, s32[8]{0:T(128)S(1)}, s32[]{:T(128)}, /*index=5*/f32[12,19,256]{2,1,0:T(8,128)S(1)},...) while((s32[]{:T(128)}, f32[16,256]{1,0:T(8,128)S(1)}, ...), condition=%wide.region_14.14_spmd, body=%wide.region_13.13_spmd.sunk | while | flops 13250570 | bytes 67841 | solution.py:129
  309.4 18.8 %while.92 = (s32[]{:T(128)}, f32[16,256]{1,0:T(8,128)S(1)}, s32[]{:T(128)}, s32[8]{0:T(128)S(1)}, s32[]{:T(128)}, /*index=5*/f32[12,19,256]{2,1,0:T(8,128)S(1)},...) while((s32[]{:T(128)}, f32[16,256]{1,0:T(8,128)S(1)}, ...), condition=%wide.region_14.14_spmd, body=%wide.region_13.13_spmd.sunk | while | flops 13250570 | bytes 67841 | solution.py:129
  (312 shorter events, 78.5 us)
Async XLA Ops:
  0.0 0.8 copy-start.3
  4.7 0.8 copy-start.2
  9.0 234.7 %collective-permute-start.1 = (f32[19,1024]{1,0:T(8,128)S(1)}, f32[19,1024]{1,0:T(8,128)S(1)}, u32[]{:S(2)}, u32[]{:S(2)}) collective-permute-start(f32[19,1024]{1,0:T(8,128)S(1)} %pad_maximum_fusion.1), channel_id=1, source_target_pairs={{1,0},{2,1},{3,2},{4,3},{5,4},{6,5},{7,6},{8,7},{9,8},{10,9},{11,1... | collective-permute-start | bytes 233480 | tf_op jit(solution)/shard_map/ppermute | solution.py:21
  21.9 221.8 %collective-permute-start = (f32[19,1024]{1,0:T(8,128)S(1)}, f32[19,1024]{1,0:T(8,128)S(1)}, u32[]{:S(2)}, u32[]{:S(2)}) collective-permute-start(f32[19,1024]{1,0:T(8,128)S(1)} %pad_maximum_fusion.1), channel_id=1, source_target_pairs={{0,1},{1,2},{2,3},{3,4},{4,5},{5,6},{6,7},{7,8},{8,9},{9,10},{10,1... | collective-permute-start | bytes 233480 | tf_op jit(solution)/shard_map/ppermute | solution.py:19
  23.9 0.7 copy-start
  52.1 0.7 copy-start.1
  244.0 0.7 copy-start.4
where the time goes:
time: 331 us; the launch traced here: 329 us
  blocking collectives  172 us (52%)
  local copies, waits for them, and re-layouts  55.4 us (17%)
  loops' own time  45.1 us (14%)
  matrix products  39.9 us (12%)
  starting transfers between devices  14.8 us (4%)
    psum x1, blocking collectives, body(): group_weights = lax.psum(raised, 'dev')  90.3 us
    another operation x4, loops' own time, near_leaf(): return lax.fori_loop(0, slot_total, one_slot, direct)  41.7 us
    dot_general x102, matrix products, translate(): jnp.dot(values, kernel_tile(source, target), precision=lax.Precision.HIGH...  39.9 us
    all_gather x1, blocking collectives, body(): lax.all_gather(block_weights, 'dev', axis=1, tiled=True)  30.2 us
    all_gather x1, blocking collectives, body(): lax.all_gather(skel_block, 'dev', axis=1, tiled=True)  27.1 us
    all_gather x1, blocking collectives, body(): lax.all_gather(group_weights, 'grp', axis=1, tiled=True)  24.5 us
    dynamic_slice x32, local copies, waits for them, and re-layouts, one_slot(): row_nbr[slot_index] - first_leaf  19.9 us
    slice x138, local copies, waits for them, and re-layouts, kernel_tile(): distance = (source[0][:, None] - target[0][None, :]) ** 2  18.6 us
  transfers between devices with their start and end apart: 2, of which 0 were waited for; matrix products, arithmetic and copies ran while one was open for 13% of the time, Pallas kernels for 0%

commit v1 on v0

--- a/solution.py
+++ b/solution.py
@@ -89,7 +89,9 @@
     group_weights = lax.psum(raised, "dev")
     group_field = far_sum(
         empty,
-        lax.all_gather(group_weights, "grp", axis=1, tiled=True),
+        jnp.concatenate(
+            lax.all_to_all(jnp.stack([group_weights] * lax.axis_size("grp")), "grp", 0, 0), axis=1
+        ),
         skel_group,
         own_group,
         group_id,

time: 331 us -> 320 us (0.967)
  the two profiles are of different devices: /device:TPU:8 before, /device:TPU:1 now
where the time goes in v1:
time: 320 us; the launch traced here: 318 us
  blocking collectives  155 us (48%)
  local copies, waits for them, and re-layouts  57.2 us (18%)
  loops' own time  45 us (14%)
  matrix products  39.9 us (12%)
  starting transfers between devices  19.3 us (6%)
    psum x1, blocking collectives, body(): group_weights = lax.psum(raised, 'dev')  93.9 us
    another operation x4, loops' own time, near_leaf(): return lax.fori_loop(0, slot_total, one_slot, direct)  41.6 us
    dot_general x102, matrix products, translate(): jnp.dot(values, kernel_tile(source, target), precision=lax.Precision.HIGH...  39.9 us
    all_gather x1, blocking collectives, body(): lax.all_gather(skel_block, 'dev', axis=1, tiled=True)  30.8 us
    all_gather x1, blocking collectives, body(): lax.all_gather(block_weights, 'dev', axis=1, tiled=True)  30.1 us
    dynamic_slice x32, local copies, waits for them, and re-layouts, one_slot(): row_nbr[slot_index] - first_leaf  20.8 us
    slice x138, local copies, waits for them, and re-layouts, kernel_tile(): distance = (source[0][:, None] - target[0][None, :]) ** 2  18.7 us
    ppermute x1, starting transfers between devices, extended_2(): lax.ppermute(head, axis, [((i + 1) % count, i) for i in range(ends)])  8.78 us
  transfers between devices with their start and end apart: 3, of which 0 were waited for; matrix products, arithmetic and copies ran while one was open for 7% of the time, Pallas kernels for 0%

profile of v1, /device:TPU:1, one launch (start us, length us, event | category | flops | bytes accessed | tf_op | source)
XLA Modules:
  0.0 317.7 jit_solution(4409680423787514675)
XLA Ops:
  0.8 0.9 copy.25
  1.7 2.8 gather_fusion.1
  5.8 2.8 gather_fusion
  9.0 8.8 %collective-permute-start.1 = (f32[19,1024]{1,0:T(8,128)S(1)}, f32[19,1024]{1,0:T(8,128)S(1)}, u32[]{:S(2)}, u32[]{:S(2)}) collective-permute-start(f32[19,1024]{1,0:T(8,128)S(1)} %pad_maximum_fusion.1), channel_id=1, source_target_pairs={{1,0},{2,1},{3,2},{4,3},{5,4},{6,5},{7,6},{8,7},{9,8},{10,9},{11,1... | collective-permute-start | bytes 233480 | tf_op jit(solution)/shard_map/ppermute | solution.py:21
  17.8 1.9 collective-permute-start
  21.6 1.6 while.85
  23.2 1.7 while.86
  26.3 93.9 %psum.7 = f32[16,256]{1,0:T(8,128)S(1)} all-reduce(f32[16,256]{1,0:T(8,128)S(1)} %convolution_multiply_fusion.7), channel_id=1, replica_groups=mesh['grp'=16,'dev'=32] {'dev'}, use_global_device_ids=true, to_apply=%region_7.8 | all-reduce | flops 4096 | bytes 32768 | tf_op jit(solution)/shard_map/psum | solution.py:89
  120.8 8.6 %all-to-all-start = ((f32[16,16,256]{2,1,0:T(8,128)}), f32[16,16,256]{2,1,0:T(8,128)S(1)}, u32[]{:S(2)}, u32[]{:S(2)}) async-start(f32[16,16,256]{2,1,0:T(8,128)} %stack.2), calls=%async_computation | async-start | bytes 524288 | tf_op jit(solution)/shard_map/all_to_all | solution.py:93
  129.5 30.8 %all_gather.7 = f32[3,8192]{1,0:T(4,128)S(1)} all-gather(f32[3,256]{1,0:T(4,128)S(1)} %get-tuple-element.1439), channel_id=1, replica_groups=mesh['grp'=16,'dev'=32] {'dev'}, dimensions={1}, use_global_device_ids=true | all-gather | bytes 101376 | tf_op jit(solution)/shard_map/all_gather | solution.py:104
  160.3 30.1 %all_gather.6 = f32[16,8192]{1,0:T(8,128)S(1)} all-gather(f32[16,256]{1,0:T(8,128)S(1)} %reduce_sum.9), channel_id=1, replica_groups=mesh['grp'=16,'dev'=32] {'dev'}, dimensions={1}, use_global_device_ids=true | all-gather | bytes 540672 | tf_op jit(solution)/shard_map/all_gather | solution.py:103
  190.4 17.0 %while.90 = (s32[]{:T(128)}, f32[16,256]{1,0:T(8,128)S(1)}, f32[16,8192]{1,0:T(8,128)S(1)}, f32[3,8192]{1,0:T(4,128)S(1)}, f32[3,256]{1,0:T(4,128)S(1)}, /*index...) while((s32[]{:T(128)}, f32[16,256]{1,0:T(8,128)S(1)}, ...), condition=%wide.region_6.7_spmd.clone, body=%wide.region_5.6_spmd.clone.sunk | while | flops 13250586 | bytes 68032 | solution.py:57
  208.4 21.3 %while.91 = (s32[]{:T(128)}, f32[16,256]{1,0:T(8,128)S(1)}, f32[16,4096]{1,0:T(8,128)S(1)}, f32[3,4096]{1,0:T(4,128)}, f32[3,256]{1,0:T(4,128)S(1)}, /*index=5*/...) while((s32[]{:T(128)}, f32[16,256]{1,0:T(8,128)S(1)}, ...), condition=%wide.region_9.10_spmd.clone, body=%wide.region_8.9_spmd.clone.sunk | while | flops 13250586 | bytes 68032 | solution.py:57
  208.5 0.9 constant_dynamic-slice_fusion.38
  209.8 0.9 constant_dynamic-slice_fusion.38
  211.1 0.9 constant_dynamic-slice_fusion.38
  212.5 0.9 constant_dynamic-slice_fusion.38
  213.8 0.9 constant_dynamic-slice_fusion.38
  215.1 0.9 constant_dynamic-slice_fusion.38
  216.5 0.9 constant_dynamic-slice_fusion.38
  217.8 0.9 constant_dynamic-slice_fusion.38
  219.1 0.9 constant_dynamic-slice_fusion.38
  221.8 0.9 constant_dynamic-slice_fusion.38
  223.1 0.9 constant_dynamic-slice_fusion.38
  225.8 0.9 constant_dynamic-slice_fusion.38
  228.5 0.9 constant_dynamic-slice_fusion.38
  230.2 1.8 while.87
  232.7 84.4 %while.89 = (s32[]{:T(128)}, f32[4,16,256]{2,1,0:T(8,128)S(1)}, f32[4,16,256]{2,1,0:T(8,128)S(1)}, f32[4,3,256]{2,1,0:T(4,128)S(1)}, f32[4,16,256]{2,1,0:T(8,128...) while((s32[]{:T(128)}, f32[4,16,256]{2,1,0:T(8,128)S(1)}, ...), condition=%wide.region_15.16_spmd, body=%wide.region_12.15_spmd.sunk | while | flops 39735312 | bytes 213682 | solution.py:133
  234.8 19.0 %while.92 = (s32[]{:T(128)}, f32[16,256]{1,0:T(8,128)S(1)}, s32[]{:T(128)}, s32[8]{0:T(128)S(1)}, s32[]{:T(128)}, /*index=5*/f32[12,19,256]{2,1,0:T(8,128)S(1)},...) while((s32[]{:T(128)}, f32[16,256]{1,0:T(8,128)S(1)}, ...), condition=%wide.region_14.14_spmd, body=%wide.region_13.13_spmd.sunk | while | flops 13250570 | bytes 67841 | solution.py:131
  255.9 19.0 %while.92 = (s32[]{:T(128)}, f32[16,256]{1,0:T(8,128)S(1)}, s32[]{:T(128)}, s32[8]{0:T(128)S(1)}, s32[]{:T(128)}, /*index=5*/f32[12,19,256]{2,1,0:T(8,128)S(1)},...) while((s32[]{:T(128)}, f32[16,256]{1,0:T(8,128)S(1)}, ...), condition=%wide.region_14.14_spmd, body=%wide.region_13.13_spmd.sunk | while | flops 13250570 | bytes 67841 | solution.py:131
  277.0 19.0 %while.92 = (s32[]{:T(128)}, f32[16,256]{1,0:T(8,128)S(1)}, s32[]{:T(128)}, s32[8]{0:T(128)S(1)}, s32[]{:T(128)}, /*index=5*/f32[12,19,256]{2,1,0:T(8,128)S(1)},...) while((s32[]{:T(128)}, f32[16,256]{1,0:T(8,128)S(1)}, ...), condition=%wide.region_14.14_spmd, body=%wide.region_13.13_spmd.sunk | while | flops 13250570 | bytes 67841 | solution.py:131
  298.1 19.0 %while.92 = (s32[]{:T(128)}, f32[16,256]{1,0:T(8,128)S(1)}, s32[]{:T(128)}, s32[8]{0:T(128)S(1)}, s32[]{:T(128)}, /*index=5*/f32[12,19,256]{2,1,0:T(8,128)S(1)},...) while((s32[]{:T(128)}, f32[16,256]{1,0:T(8,128)S(1)}, ...), condition=%wide.region_14.14_spmd, body=%wide.region_13.13_spmd.sunk | while | flops 13250570 | bytes 67841 | solution.py:131
  (315 shorter events, 80.3 us)
Async XLA Ops:
  0.0 0.8 copy-start.3
  4.8 0.8 copy-start.2
  9.0 199.1 %collective-permute-start.1 = (f32[19,1024]{1,0:T(8,128)S(1)}, f32[19,1024]{1,0:T(8,128)S(1)}, u32[]{:S(2)}, u32[]{:S(2)}) collective-permute-start(f32[19,1024]{1,0:T(8,128)S(1)} %pad_maximum_fusion.1), channel_id=1, source_target_pairs={{1,0},{2,1},{3,2},{4,3},{5,4},{6,5},{7,6},{8,7},{9,8},{10,9},{11,1... | collective-permute-start | bytes 233480 | tf_op jit(solution)/shard_map/ppermute | solution.py:21
  17.8 190.3 %collective-permute-start = (f32[19,1024]{1,0:T(8,128)S(1)}, f32[19,1024]{1,0:T(8,128)S(1)}, u32[]{:S(2)}, u32[]{:S(2)}) collective-permute-start(f32[19,1024]{1,0:T(8,128)S(1)} %pad_maximum_fusion.1), channel_id=1, source_target_pairs={{0,1},{1,2},{2,3},{3,4},{4,5},{5,6},{6,7},{7,8},{8,9},{9,10},{10,1... | collective-permute-start | bytes 233480 | tf_op jit(solution)/shard_map/ppermute | solution.py:19
  19.8 0.7 copy-start
  20.8 0.7 copy-start.1
  120.8 87.6 %all-to-all-start = ((f32[16,16,256]{2,1,0:T(8,128)}), f32[16,16,256]{2,1,0:T(8,128)S(1)}, u32[]{:S(2)}, u32[]{:S(2)}) async-start(f32[16,16,256]{2,1,0:T(8,128)} %stack.2), calls=%async_computation | async-start | bytes 524288 | tf_op jit(solution)/shard_map/all_to_all | solution.py:93
  232.0 0.7 copy-start.4
